TPU v7x, 32 devices: a whole 2x2x4 slice. The times are simulated.
32 devices in a mesh: grp: 4 (over y, x), line: 8 (over z, core).
Axes of the slice: x: 2, y: 2, z: 4, core: 2. Of those that a mesh axis runs over, the one named last changes fastest.
Arguments:
- velocity: bfloat16 [3, 1536, 96, 512], P(None, 'line', 'grp'), may hold values from -6 to 6
- vorticity: bfloat16 [3, 1536, 96, 512], P(None, 'line', 'grp'), may hold values from -6 to 6
- wall_velocity: float32 [2, 256, 96, 1536], P(None, ('grp', 'line')), may hold values from -6 to 6
- wall_vorticity: float32 [2, 256, 96, 1536], P(None, ('grp', 'line')), may hold values from -6 to 6
- keep_mask: int32 [256, 96], P(('grp', 'line')), may hold values from 0 to 1, as said below
- derivative_band: float32 [7, 1536], replicated, may hold values from -3 to 3
- eigenvalues: float32 [1536], replicated, may hold values from 0.25 to 4
- eigenbasis: float32 [1536, 1536], replicated, may hold values from -0.15625 to 0.15625
Outputs:
- new_velocity: float32 [2, 256, 96, 1536], P(None, ('grp', 'line'))
- new_vorticity: float32 [2, 256, 96, 1536], P(None, ('grp', 'line'))
Inputs may be any that keep to these rules, and one draw needn't show every extreme that they name: keep_mask is 0 wherever kx >= 170, or 32 <= kz < 64.
All inputs are finite; a program needn't handle non-finite values.
Results may differ from a plain program's by a relative error of at most 0.0003.
Values sent between devices are 32-bit elements; how exact they have to be, the bound alone decides.
A program may use at most 384 MiB of HBM per device.

v0:
```python
import math
import jax
import jax.numpy as jnp
from jax import lax
from jax.sharding import PartitionSpec as P

HIGHEST_PRECISION = lax.Precision.HIGHEST


def phase_table(indices, points):
    index_cols = jnp.arange(points, dtype=jnp.int32)[None, :]
    phase_angle = (indices[:, None] * index_cols % points).astype(jnp.float32) * (
        2.0 * math.pi / points
    )
    norm_scale = 1.0 / math.sqrt(points)
    return (jnp.cos(phase_angle) * norm_scale, jnp.sin(phase_angle) * norm_scale)


def signed_wave(indices, points):
    signed_index = jnp.where(indices < points // 2, indices, indices - points)
    return signed_index.astype(jnp.float32) / (points / 2.0)


def curl_terms(spectra, stream_wave, span_wave):
    slope_source = jnp.stack(
        [
            -stream_wave * spectra[0, 1] - span_wave * spectra[2, 1],
            stream_wave * spectra[0, 0] + span_wave * spectra[2, 0],
        ]
    )
    normal_term = jnp.stack(
        [
            -span_wave * spectra[0, 1] + stream_wave * spectra[2, 1],
            span_wave * spectra[0, 0] - stream_wave * spectra[2, 0],
        ]
    )
    return (slope_source, normal_term)


def banded(padded, band_rows, extent):
    summed = band_rows[0] * padded[..., 0:extent]
    for offset in range(1, 7):
        summed = summed + band_rows[offset] * padded[..., offset : offset + extent]
    return summed


def local(
    velocity,
    vorticity,
    wall_velocity,
    wall_vorticity,
    keep_mask,
    derivative_band,
    eigenvalues,
    eigenbasis,
):
    group_count = lax.axis_size("grp")
    line_count = lax.axis_size("line")
    group_index = lax.axis_index("grp")
    line_index = lax.axis_index("line")
    moving = velocity.astype(jnp.float32)
    turning = vorticity.astype(jnp.float32)
    lamb_vector = jnp.stack(
        [
            moving[1] * turning[2] - moving[2] * turning[1],
            moving[2] * turning[0] - moving[0] * turning[2],
            moving[0] * turning[1] - moving[1] * turning[0],
        ]
    )
    slab_depth = lamb_vector.shape[1]
    span_share = lamb_vector.shape[2]
    stream_points = lamb_vector.shape[3]
    span_points = span_share * group_count
    stream_modes = stream_points // 2
    group_modes = stream_modes // group_count
    line_modes = group_modes // line_count
    span_keep = span_points // 3
    wall_points = wall_velocity.shape[3]
    span_list = jnp.concatenate(
        [
            jnp.arange(span_keep, dtype=jnp.int32),
            jnp.arange(span_points - span_keep, span_points, dtype=jnp.int32),
        ]
    )
    span_count = span_list.shape[0]
    stream_cosine, stream_sine = phase_table(
        jnp.arange(stream_modes, dtype=jnp.int32), stream_points
    )
    stream_table = jnp.stack(
        [
            stream_cosine.reshape(group_count, group_modes, stream_points),
            -stream_sine.reshape(group_count, group_modes, stream_points),
        ],
        1,
    )
    stream_table = stream_table.reshape(2 * stream_modes, stream_points)
    stream_spectra = jnp.einsum(
        "rx,cx->rc",
        lamb_vector.reshape(-1, stream_points),
        stream_table,
        precision=HIGHEST_PRECISION,
    )
    stream_spectra = stream_spectra.reshape(3, slab_depth, span_share, 2 * stream_modes)
    span_cosine, span_sine = phase_table(span_list, span_points)
    planes = lax.all_to_all(stream_spectra, "grp", split_axis=3, concat_axis=2, tiled=True)
    count_items = planes.shape[1]
    cosine_part = jnp.einsum("qz,fnzc->fcqn", span_cosine, planes, precision=HIGHEST_PRECISION)
    sine_part = jnp.einsum("qz,fnzc->fcqn", span_sine, planes, precision=HIGHEST_PRECISION)
    cosine_part = cosine_part.reshape(3, 2, group_modes, span_count, count_items)
    sine_part = sine_part.reshape(3, 2, group_modes, span_count, count_items)
    real_part = cosine_part[:, 0] + sine_part[:, 1]
    imag_part = cosine_part[:, 1] - sine_part[:, 0]
    local_modes = jnp.stack([real_part, imag_part], 1)
    span_wave = signed_wave(span_list, span_points)[:, None]
    device_modes = (group_index * line_count + line_index) * line_modes + jnp.arange(
        line_modes, dtype=jnp.int32
    )
    device_wave = (device_modes.astype(jnp.float32) / stream_modes)[:, None, None]
    whole_lines = lax.all_to_all(local_modes, "line", split_axis=2, concat_axis=4, tiled=True)
    wave_square = device_wave * device_wave + span_wave * span_wave
    slope_source, normal_term = curl_terms(whole_lines, device_wave, span_wave)
    padded = jnp.pad(slope_source, ((0, 0), (0, 0), (0, 0), (3, 3)))
    arrived = jnp.stack(
        [wave_square * whole_lines[1] - banded(padded, derivative_band, wall_points), normal_term]
    )
    middle = jnp.zeros((2, 2, line_modes, span_points - 2 * span_keep, wall_points), jnp.float32)
    arrived = jnp.concatenate(
        [arrived[:, :, :, :span_keep], middle, arrived[:, :, :, span_keep:]], 3
    )
    keep_weight = keep_mask.astype(jnp.float32)[:, :, None]
    right_side = jnp.stack([wall_velocity, wall_vorticity]) + keep_weight * arrived
    full_wave = signed_wave(jnp.arange(span_points, dtype=jnp.int32), span_points)[:, None]
    full_square = device_wave * device_wave + full_wave * full_wave
    eigen_coeffs = jnp.einsum(
        "fpkqy,yj->fpkqj", right_side, eigenbasis, precision=HIGHEST_PRECISION
    )
    eigen_coeffs = eigen_coeffs / (eigenvalues + full_square)
    solved = jnp.einsum("fpkqj,yj->fpkqy", eigen_coeffs, eigenbasis, precision=HIGHEST_PRECISION)
    return (solved[0], solved[1])


def solution(mesh):
    placed = (
        P(None, "line", "grp", None),
        P(None, "line", "grp", None),
        P(None, ("grp", "line"), None, None),
        P(None, ("grp", "line"), None, None),
        P(("grp", "line"), None),
        P(),
        P(),
        P(),
    )
    return jax.shard_map(
        local,
        mesh=mesh,
        in_specs=placed,
        out_specs=(P(None, ("grp", "line"), None, None), P(None, ("grp", "line"), None, None)),
        check_vma=False,
    )
```

profile of v0, /device:TPU:0, one launch (start us, length us, event | category | flops | bytes accessed | tf_op | source)
XLA Modules:
  0.0 1655.5 jit_solution(10274515562087793496)
XLA Ops:
  0.6 0.0 copy-start
  0.7 17.1 %convert_element_type.71 = f32[3,192,24,512]{3,2,1,0:T(8,128)} convert(bf16[3,192,24,512]{3,2,1,0:T(8,128)(2,1)} %param.8) | non-fusion elementwise | flops 7077888 | bytes 42467328 | tf_op jit(solution)/shard_map/convert_element_type | solution.py:61
  17.7 2.4 copy-done
  20.1 10.3 convert_element_type.72
  30.4 2.2 cosine_multiply_fusion
  32.6 30.8 %multiply_subtract_fusion.2 = (f32[1,192,24,512]{3,2,1,0:T(8,128)}, f32[1,192,24,512]{3,2,1,0:T(8,128)}, f32[1,192,24,512]{3,2,1,0:T(8,128)}) fusion(f32[3,192,24,512]{3,2,1,0:T(8,128)} %convert_element_type.72, f32[3,192,24,512]{3,2,1,0:T(8,128)} %convert_element_type.71), kind=kLoop, calls=%fused_computation.37 | loop fusion | flops 21233664 | bytes 84934656 | tf_op jit(solution)/shard_map/sub | solution.py:65
  63.4 0.1 pad_maximum_fusion.2
  63.5 51.6 %fusion = f32[3,192,24,512]{3,2,1,0:T(8,128)} fusion(f32[512,512,1,1]{1,0,3,2:T(8,128)S(1)} %bitcast.85, f32[1,192,24,512]{3,2,1,0:T(8,128)} %get-tuple-element.14, f32[1,192,24,512]{3,2,1,0:T(8,128)} %get-tuple-element.13, f32[1,192,24,512]{3,2,1,0:T(8,128)} %get-tuple-element.12), kind=kOutput, calls=%fused_computation | convolution fusion | flops 43500699648 | bytes 57671680 | tf_op jit(solution)/shard_map/rx,cx->rc/dot_general | solution.py:97
  115.1 36.9 %copy.28 = f32[3,192,24,512]{1,2,0,3:T(8,128)} copy(f32[3,192,24,512]{3,2,1,0:T(8,128)} %fusion) | data formatting | bytes 56623104 | tf_op jit(solution)/shard_map/rx,cx->rc/dot_general | solution.py:97
  152.0 11.0 all-to-all-start
  163.0 0.1 fusion.82
  163.1 408.4 %all-to-all-done = f32[3,192,24,512]{1,2,0,3:T(8,128)} async-done(((f32[3,192,24,512]{1,2,0,3:T(8,128)}), f32[3,192,24,512]{1,2,0,3:T(8,128)}, u32[]{:S(2)}, u32[]{:S(2)}) %all-to-all-start) | async-done | bytes 28311584 | tf_op jit(solution)/shard_map/all_to_all | solution.py:105
  571.6 34.4 %copy.29 = f32[3,192,24,4,128]{4,2,3,1,0:T(8,128)} copy(f32[3,192,24,4,128]{1,2,0,4,3:T(8,128)} %bitcast.5) | data formatting | bytes 56623104 | tf_op jit(solution)/shard_map/all_to_all | solution.py:105
  606.0 26.2 %convolution_bitcast_fusion.1 = f32[3,128,64,192]{1,2,3,0:T(8,128)} fusion(f32[3,192,96,128]{3,2,1,0:T(8,128)} %bitcast.80, s32[64]{0:T(128)S(1)} %get-tuple-element.11), kind=kOutput, calls=%fused_computation.40 | convolution fusion | flops 5435879424 | bytes 47186176 | tf_op jit(solution)/shard_map/qz,fnzc->fcqn/dot_general | solution.py:107
  632.3 26.2 %convolution_bitcast_fusion = f32[3,128,64,192]{1,2,3,0:T(8,128)} fusion(f32[3,192,96,128]{3,2,1,0:T(8,128)} %bitcast.81, s32[64]{0:T(128)S(1)} %get-tuple-element.11), kind=kOutput, calls=%fused_computation.39 | convolution fusion | flops 5435879424 | bytes 47186176 | tf_op jit(solution)/shard_map/qz,fnzc->fcqn/dot_general | solution.py:108
  658.4 25.1 %copy.30 = f32[3,128,64,192]{3,2,1,0:T(8,128)} copy(f32[3,128,64,192]{1,2,3,0:T(8,128)} %convolution_bitcast_fusion.1) | data formatting | bytes 37748736 | tf_op jit(solution)/shard_map/qz,fnzc->fcqn/transpose | solution.py:107
  683.5 25.1 %copy.31 = f32[3,128,64,192]{3,2,1,0:T(8,128)} copy(f32[3,128,64,192]{1,2,3,0:T(8,128)} %convolution_bitcast_fusion) | data formatting | bytes 37748736 | tf_op jit(solution)/shard_map/qz,fnzc->fcqn/transpose | solution.py:108
  708.6 27.5 %slice_add_fusion = (f32[3,1,64,64,192]{4,3,2,1,0:T(8,128)}, f32[3,1,64,64,192]{4,3,2,1,0:T(8,128)}) fusion(f32[3,2,64,64,192]{4,3,2,1,0:T(8,128)} %bitcast.83, f32[3,2,64,64,192]{4,3,2,1,0:T(8,128)} %bitcast.82), kind=kLoop, calls=%fused_computation.24 | loop fusion | flops 4718592 | bytes 56623104 | tf_op jit(solution)/shard_map/add | solution.py:111
  736.1 9.4 pad_maximum_fusion
  745.5 8.6 copy.32
  754.2 0.0 copy-start.3
  754.2 0.0 copy-start.1
  754.2 0.0 copy-start.2
  754.2 6.6 all-to-all-start.1
  760.8 0.0 copy-done.3
  760.8 0.1 pad.6.clone
  760.9 0.0 copy-done.1
  760.9 0.1 slice_reduce_fusion.6
  761.0 0.1 broadcast_add_fusion.2
  761.1 0.1 broadcast_add_fusion.1
  761.2 0.0 copy-done.2
  761.2 2.6 broadcast_add_fusion
  763.7 540.4 %all-to-all-done.1 = f32[3,2,64,64,192]{4,3,1,0,2:T(8,128)} async-done(((f32[3,2,64,64,192]{4,3,1,0,2:T(8,128)}), f32[3,2,64,64,192]{4,3,1,0,2:T(8,128)}, u32[]{:S(2)}, u32[]{:S(2)}) %all-to-all-start.1) | async-done | bytes 18874400 | tf_op jit(solution)/shard_map/all_to_all | solution.py:119
  1304.1 26.5 %copy.35 = f32[3,2,8,64,8,192]{5,4,3,2,1,0:T(8,128)} copy(f32[3,2,8,64,8,192]{5,3,1,0,2,4:T(8,128)} %bitcast.20) | data formatting | bytes 37748736 | tf_op jit(solution)/shard_map/all_to_all | solution.py:119
  1330.7 25.3 %all_to_all.33 = f32[3,2,8,64,1536]{4,3,2,1,0:T(8,128)} reshape(f32[3,2,8,64,8,192]{5,4,3,2,1,0:T(8,128)} %copy.35) | data formatting | bytes 37748736 | tf_op jit(solution)/shard_map/all_to_all | solution.py:119
  1355.9 17.5 %copy.33 = f32[3,2,64,64,192]{4,3,2,1,0:T(8,128)} copy(f32[3,2,64,64,192]{4,3,1,0,2:T(8,128)} %all-to-all-done.1) | data formatting | bytes 37748736 | tf_op jit(solution)/shard_map/all_to_all | solution.py:119
  1373.5 4.0 slice.150
  1377.5 9.9 copy.34
  1387.4 9.5 squeeze.14
  1396.9 5.6 multiply_add_fusion.1
  1402.5 3.1 pad_maximum_fusion.1
  1405.6 3.1 maximum_bitcast_fusion
  1408.8 23.5 %subtract_bitcast_fusion = f32[1,2,8,64,1536]{4,3,2,1,0:T(8,128)} fusion(f32[2,8,64,1536]{3,2,1,0:T(8,128)} %pad_maximum_fusion.1, f32[2,8,64,1536]{3,2,1,0:T(8,128)} %squeeze.14, f32[1536]{0:T(1024)S(1)} %get-tuple-element.7, f32[1536]{0:T(1024)S(1)} %get-tuple-element.8, f32[1536]{0:T(1024)S(1)} %get-tuple-element.3, f32[1536]{0:T(1024)S(1)} %get-tuple-element.4, ...), kind=kLoop, calls=%fused_computation.44 | loop fusion | flops 23592960 | bytes 18919424 | tf_op jit(solution)/shard_map/stack | solution.py:123
  1432.3 6.3 fusion.28
  1438.6 105.2 %fusion.9 = f32[2,2,8,96,1536]{4,3,2,1,0:T(8,128)} fusion(f32[1,2,8,64,1536]{4,3,2,1,0:T(8,128)} %maximum_bitcast_fusion, f32[1,2,8,64,1536]{4,3,2,1,0:T(8,128)} %subtract_bitcast_fusion, f32[1,2,8,96,1536]{4,3,2,1,0:T(8,128)} %bitcast.86, f32[1,2,8,96,1536]{4,3,2,1,0:T(8,128)} %bitcast.87, f32[2,2,8,32,1536]{4,3,2,1,0:T(8,128)} %fusion.28, ...), kind=kOutput, calls=%fused_computation.11 | convolution fusion | flops 87015555072 | bytes 66063744 | tf_op jit(solution)/shard_map/fpkqy,yj->fpkqj/dot_general | solution.py:134
  1543.8 99.0 %fusion.19 = f32[2,2,8,96,1536]{4,3,2,1,0:T(8,128)} fusion(f32[2,2,8,96,1536]{4,3,2,1,0:T(8,128)} %fusion.9, f32[1536,1536]{1,0:T(8,128)} %param.15, f32[8,96,1536]{2,1,0:T(8,128)} %broadcast_add_fusion), kind=kOutput, calls=%fused_computation.21 | convolution fusion | flops 86977806336 | bytes 51904512 | tf_op jit(solution)/shard_map/fpkqj,yj->fpkqy/dot_general | solution.py:138
  1642.7 12.6 slice_bitcast_fusion
  (9 shorter events, 0.0 us)
Async XLA Ops:
  0.6 19.5 %copy-start = (bf16[3,192,24,512]{3,2,1,0:T(8,128)(2,1)S(1)}, bf16[3,192,24,512]{3,2,1,0:T(8,128)(2,1)}, u32[]{:S(2)}) copy-start(bf16[3,192,24,512]{3,2,1,0:T(8,128)(2,1)} %param.9) | copy-start | bytes 42467332
  152.0 419.6 %all-to-all-start = ((f32[3,192,24,512]{1,2,0,3:T(8,128)}), f32[3,192,24,512]{1,2,0,3:T(8,128)}, u32[]{:S(2)}, u32[]{:S(2)}) async-start(f32[3,192,24,512]{1,2,0,3:T(8,128)} %copy.28), calls=%async_computation | async-start | bytes 75497472 | tf_op jit(solution)/shard_map/all_to_all | solution.py:105
  754.2 6.6 copy-start.3
  754.2 6.7 copy-start.1
  754.2 7.0 copy-start.2
  754.2 550.0 %all-to-all-start.1 = ((f32[3,2,64,64,192]{4,3,1,0,2:T(8,128)}), f32[3,2,64,64,192]{4,3,1,0,2:T(8,128)}, u32[]{:S(2)}, u32[]{:S(2)}) async-start(f32[3,2,64,64,192]{4,3,1,0,2:T(8,128)} %copy.32), calls=%async_computation.1 | async-start | bytes 50331648 | tf_op jit(solution)/shard_map/all_to_all | solution.py:119
where the time goes:
time: 1660 us
  waiting for transfers between devices  949 us (57%)
  matrix products  308 us (19%)
  local copies, waits for them, and re-layouts  238 us (14%)
  other arithmetic  142 us (9%)
  starting transfers between devices  17.6 us (1%)
    all_to_all x1, waiting for transfers between devices, local(): lax.all_to_all(local_modes, 'line', split_axis=2, concat_axis=4, tiled=True)  540 us
    all_to_all x1, waiting for transfers between devices, local(): lax.all_to_all(stream_spectra, 'grp', split_axis=3, concat_axis=2, tiled=...  408 us
    dot_general x1, matrix products, local(): jnp.einsum('fpkqy,yj->fpkqj', right_side, eigenbasis, precision=HIGHEST_P...  105 us
    dot_general x1, matrix products, local(): jnp.einsum('fpkqj,yj->fpkqy', eigen_coeffs, eigenbasis, precision=HIGHEST...  99 us
    all_to_all x3, local copies, waits for them, and re-layouts, local(): lax.all_to_all(local_modes, 'line', split_axis=2, concat_axis=4, tiled=True)  69.3 us
    dot_general x1, matrix products, local(): jnp.einsum('rx,cx->rc', lamb_vector.reshape(-1, stream_points), stream_ta...  51.6 us
    dot_general x1, local copies, waits for them, and re-layouts, local(): jnp.einsum('rx,cx->rc', lamb_vector.reshape(-1, stream_points), stream_ta...  36.9 us
    all_to_all x1, local copies, waits for them, and re-layouts, local(): lax.all_to_all(stream_spectra, 'grp', split_axis=3, concat_axis=2, tiled=...  34.4 us
  transfers between devices with their start and end apart: 2, of which 2 were waited for; matrix products, arithmetic and copies ran while one was open for 0% of the time, Pallas kernels for 0%

commit v1 on v0

--- a/solution.py
+++ b/solution.py
@@ -102,7 +102,12 @@
     )
     stream_spectra = stream_spectra.reshape(3, slab_depth, span_share, 2 * stream_modes)
     span_cosine, span_sine = phase_table(span_list, span_points)
-    planes = lax.all_to_all(stream_spectra, "grp", split_axis=3, concat_axis=2, tiled=True)
+    planes = jnp.concatenate(
+        lax.all_to_all(
+            jnp.stack(jnp.split(stream_spectra, lax.axis_size("grp"), axis=3)), "grp", 0, 0
+        ),
+        axis=2,
+    )
     count_items = planes.shape[1]
     cosine_part = jnp.einsum("qz,fnzc->fcqn", span_cosine, planes, precision=HIGHEST_PRECISION)
     sine_part = jnp.einsum("qz,fnzc->fcqn", span_sine, planes, precision=HIGHEST_PRECISION)

time: 1660 us -> 1550 us (0.934)
  waiting for transfers between devices: 949 us -> 848 us
  local copies, waits for them, and re-layouts: 238 us -> 208 us
  other arithmetic: 142 us -> 162 us
    all_to_all x1, waiting for transfers between devices: 408 us -> 307 us  [local(): lax.all_to_all(jnp.stack(jnp.split(stream_spectra, lax.axis_size('grp'),...]
    dot_general x1 -> x0, local copies, waits for them, and re-layouts: 36.9 us -> none  [local(): jnp.einsum('rx,cx->rc', lamb_vector.reshape(-1, stream_points), stream_ta...]
    all_to_all x1 -> x0, local copies, waits for them, and re-layouts: 34.4 us -> none  [local(): lax.all_to_all(stream_spectra, 'grp', split_axis=3, concat_axis=2, tiled=...]
    reshape x0 -> x1, local copies, waits for them, and re-layouts: none -> 21.4 us  [local(): jnp.concatenate(lax.all_to_all(jnp.stack(jnp.split(stream_spectra, lax.ax...]
    another operation x0 -> x1, other arithmetic: none -> 20.9 us  [local(): jnp.stack(jnp.split(stream_spectra, lax.axis_size('grp'), axis=3))]
    another operation x0 -> x1, local copies, waits for them, and re-layouts: none -> 20.3 us  [local(): jnp.stack(jnp.split(stream_spectra, lax.axis_size('grp'), axis=3))]
where the time goes in v1:
time: 1550 us; the launch traced here: 1540 us
  waiting for transfers between devices  848 us (55%)
  matrix products  308 us (20%)
  local copies, waits for them, and re-layouts  208 us (13%)
  other arithmetic  162 us (10%)
  starting transfers between devices  16 us (1%)
    all_to_all x1, waiting for transfers between devices, local(): lax.all_to_all(local_modes, 'line', split_axis=2, concat_axis=4, tiled=True)  540 us
    all_to_all x1, waiting for transfers between devices, local(): lax.all_to_all(jnp.stack(jnp.split(stream_spectra, lax.axis_size('grp'),...  307 us
    dot_general x1, matrix products, local(): jnp.einsum('fpkqy,yj->fpkqj', right_side, eigenbasis, precision=HIGHEST_P...  105 us
    dot_general x1, matrix products, local(): jnp.einsum('fpkqj,yj->fpkqy', eigen_coeffs, eigenbasis, precision=HIGHEST...  99 us
    all_to_all x3, local copies, waits for them, and re-layouts, local(): lax.all_to_all(local_modes, 'line', split_axis=2, concat_axis=4, tiled=True)  69.3 us
    dot_general x1, matrix products, local(): jnp.einsum('rx,cx->rc', lamb_vector.reshape(-1, stream_points), stream_ta...  51.6 us
    another operation x3, other arithmetic, local(): jnp.stack([wave_square * whole_lines[1] - banded(padded, derivative_band,...  31.9 us
  transfers between devices with their start and end apart: 2, of which 2 were waited for; matrix products, arithmetic and copies ran while one was open for 0% of the time, Pallas kernels for 0%

profile of v1, /device:TPU:0, one launch (start us, length us, event | category | flops | bytes accessed | tf_op | source)
XLA Modules:
  0.0 1543.0 jit_solution(3884449060299841971)
XLA Ops:
  0.6 0.0 copy-start
  0.7 17.1 %convert_element_type.71 = f32[3,192,24,512]{3,2,1,0:T(8,128)} convert(bf16[3,192,24,512]{3,2,1,0:T(8,128)(2,1)} %param.8) | non-fusion elementwise | flops 7077888 | bytes 42467328 | tf_op jit(solution)/shard_map/convert_element_type | solution.py:61
  17.7 2.4 copy-done
  20.1 10.3 convert_element_type.72
  30.4 2.2 cosine_multiply_fusion
  32.6 30.8 %multiply_subtract_fusion.2 = (f32[1,192,24,512]{3,2,1,0:T(8,128)}, f32[1,192,24,512]{3,2,1,0:T(8,128)}, f32[1,192,24,512]{3,2,1,0:T(8,128)}) fusion(f32[3,192,24,512]{3,2,1,0:T(8,128)} %convert_element_type.72, f32[3,192,24,512]{3,2,1,0:T(8,128)} %convert_element_type.71), kind=kLoop, calls=%fused_computation.38 | loop fusion | flops 21233664 | bytes 84934656 | tf_op jit(solution)/shard_map/sub | solution.py:65
  63.4 0.1 pad_maximum_fusion.3
  63.5 51.6 %fusion = f32[3,192,24,512]{3,2,1,0:T(8,128)} fusion(f32[512,512,1,1]{1,0,3,2:T(8,128)S(1)} %bitcast.91, f32[1,192,24,512]{3,2,1,0:T(8,128)} %get-tuple-element.14, f32[1,192,24,512]{3,2,1,0:T(8,128)} %get-tuple-element.13, f32[1,192,24,512]{3,2,1,0:T(8,128)} %get-tuple-element.12), kind=kOutput, calls=%fused_computation | convolution fusion | flops 43500699648 | bytes 57671680 | tf_op jit(solution)/shard_map/rx,cx->rc/dot_general | solution.py:97
  115.1 20.3 %slice_bitcast_fusion.5 = (f32[1,3,192,24,128]{4,3,2,1,0:T(8,128)}, f32[1,3,192,24,128]{4,3,2,1,0:T(8,128)}, f32[1,3,192,24,128]{4,3,2,1,0:T(8,128)}, f32[1,3,192,24,128]{4,3,2,1,0:T(8,128)}) fusion(f32[3,192,24,512]{3,2,1,0:T(8,128)} %fusion), kind=kLoop, calls=%fused_computation.45 | loop fusion | bytes 56623104 | tf_op jit(solution)/shard_map/stack | solution.py:107
  135.5 20.9 %pad_maximum_fusion = f32[4,3,192,24,128]{4,3,2,1,0:T(8,128)} fusion(f32[1,3,192,24,128]{4,3,2,1,0:T(8,128)} %get-tuple-element.18, f32[1,3,192,24,128]{4,3,2,1,0:T(8,128)} %get-tuple-element.19, f32[1,3,192,24,128]{4,3,2,1,0:T(8,128)} %get-tuple-element.20, f32[1,3,192,24,128]{4,3,2,1,0:T(8,128)} %get-tuple-element.17), kind=kLoop, calls=%fused_computation.6 | loop fusion | flops 21233664 | bytes 56623104 | tf_op jit(solution)/shard_map/stack | solution.py:107
  156.3 9.4 all-to-all-start
  165.8 0.1 fusion.82
  165.9 307.2 %all-to-all-done = f32[4,3,192,24,128]{4,3,2,1,0:T(8,128)} async-done(((f32[4,3,192,24,128]{4,3,2,1,0:T(8,128)}), f32[4,3,192,24,128]{4,3,2,1,0:T(8,128)}, u32[]{:S(2)}, u32[]{:S(2)}) %all-to-all-start) | async-done | bytes 28311584 | tf_op jit(solution)/shard_map/all_to_all | solution.py:106
  473.1 21.4 %copy.19 = f32[3,192,4,24,128]{4,3,2,1,0:T(8,128)} copy(f32[3,192,4,24,128]{4,3,1,0,2:T(8,128)} %bitcast.9) | data formatting | bytes 56623104 | tf_op jit(solution)/shard_map/reshape | solution.py:105
  494.5 26.2 %convolution_bitcast_fusion.1 = f32[3,128,64,192]{1,2,3,0:T(8,128)} fusion(f32[3,192,96,128]{3,2,1,0:T(8,128)} %bitcast.86, s32[64]{0:T(128)S(1)} %get-tuple-element.11), kind=kOutput, calls=%fused_computation.41 | convolution fusion | flops 5435879424 | bytes 47186176 | tf_op jit(solution)/shard_map/qz,fnzc->fcqn/dot_general | solution.py:112
  520.7 26.1 %convolution_bitcast_fusion = f32[3,128,64,192]{1,2,3,0:T(8,128)} fusion(f32[3,192,96,128]{3,2,1,0:T(8,128)} %bitcast.87, s32[64]{0:T(128)S(1)} %get-tuple-element.11), kind=kOutput, calls=%fused_computation.40 | convolution fusion | flops 5435879424 | bytes 47186176 | tf_op jit(solution)/shard_map/qz,fnzc->fcqn/dot_general | solution.py:113
  546.9 25.1 %copy.20 = f32[3,128,64,192]{3,2,1,0:T(8,128)} copy(f32[3,128,64,192]{1,2,3,0:T(8,128)} %convolution_bitcast_fusion.1) | data formatting | bytes 37748736 | tf_op jit(solution)/shard_map/qz,fnzc->fcqn/transpose | solution.py:112
  572.0 25.1 %copy.21 = f32[3,128,64,192]{3,2,1,0:T(8,128)} copy(f32[3,128,64,192]{1,2,3,0:T(8,128)} %convolution_bitcast_fusion) | data formatting | bytes 37748736 | tf_op jit(solution)/shard_map/qz,fnzc->fcqn/transpose | solution.py:113
  597.1 27.5 %slice_add_fusion = (f32[3,1,64,64,192]{4,3,2,1,0:T(8,128)}, f32[3,1,64,64,192]{4,3,2,1,0:T(8,128)}) fusion(f32[3,2,64,64,192]{4,3,2,1,0:T(8,128)} %bitcast.89, f32[3,2,64,64,192]{4,3,2,1,0:T(8,128)} %bitcast.88), kind=kLoop, calls=%fused_computation.25 | loop fusion | flops 4718592 | bytes 56623104 | tf_op jit(solution)/shard_map/add | solution.py:116
  624.5 9.4 pad_maximum_fusion.1
  634.0 8.6 copy.22
  642.6 0.0 copy-start.3
  642.6 0.0 copy-start.1
  642.6 0.0 copy-start.2
  642.6 6.6 all-to-all-start.1
  649.2 0.0 copy-done.3
  649.2 0.1 pad.6.clone
  649.3 0.0 copy-done.1
  649.4 0.1 slice_reduce_fusion.6
  649.5 0.1 broadcast_add_fusion.2
  649.6 0.1 broadcast_add_fusion.1
  649.6 0.0 copy-done.2
  649.6 2.6 broadcast_add_fusion
  652.2 540.4 %all-to-all-done.1 = f32[3,2,64,64,192]{4,3,1,0,2:T(8,128)} async-done(((f32[3,2,64,64,192]{4,3,1,0,2:T(8,128)}), f32[3,2,64,64,192]{4,3,1,0,2:T(8,128)}, u32[]{:S(2)}, u32[]{:S(2)}) %all-to-all-start.1) | async-done | bytes 18874400 | tf_op jit(solution)/shard_map/all_to_all | solution.py:124
  1192.6 26.5 %copy.25 = f32[3,2,8,64,8,192]{5,4,3,2,1,0:T(8,128)} copy(f32[3,2,8,64,8,192]{5,3,1,0,2,4:T(8,128)} %bitcast.22) | data formatting | bytes 37748736 | tf_op jit(solution)/shard_map/all_to_all | solution.py:124
  1219.1 25.3 %all_to_all.20 = f32[3,2,8,64,1536]{4,3,2,1,0:T(8,128)} reshape(f32[3,2,8,64,8,192]{5,4,3,2,1,0:T(8,128)} %copy.25) | data formatting | bytes 37748736 | tf_op jit(solution)/shard_map/all_to_all | solution.py:124
  1244.4 17.5 %copy.23 = f32[3,2,64,64,192]{4,3,2,1,0:T(8,128)} copy(f32[3,2,64,64,192]{4,3,1,0,2:T(8,128)} %all-to-all-done.1) | data formatting | bytes 37748736 | tf_op jit(solution)/shard_map/all_to_all | solution.py:124
  1261.9 4.0 slice.150
  1265.9 9.9 copy.24
  1275.8 9.5 squeeze.14
  1285.4 5.6 multiply_add_fusion.1
  1290.9 3.1 pad_maximum_fusion.2
  1294.1 3.1 maximum_bitcast_fusion
  1297.2 22.5 %subtract_bitcast_fusion = f32[1,2,8,64,1536]{4,3,2,1,0:T(8,128)} fusion(f32[2,8,64,1536]{3,2,1,0:T(8,128)} %pad_maximum_fusion.2, f32[2,8,64,1536]{3,2,1,0:T(8,128)} %squeeze.14, f32[1536]{0:T(1024)S(1)} %get-tuple-element.7, f32[1536]{0:T(1024)S(1)} %get-tuple-element.8, f32[1536]{0:T(1024)S(1)} %get-tuple-element.3, f32[1536]{0:T(1024)S(1)} %get-tuple-element.4, ...), kind=kLoop, calls=%fused_computation.49 | loop fusion | flops 23592960 | bytes 18919424 | tf_op jit(solution)/shard_map/stack | solution.py:128
  1319.8 6.3 fusion.28
  1326.0 105.2 %fusion.9 = f32[2,2,8,96,1536]{4,3,2,1,0:T(8,128)} fusion(f32[1,2,8,64,1536]{4,3,2,1,0:T(8,128)} %maximum_bitcast_fusion, f32[1,2,8,64,1536]{4,3,2,1,0:T(8,128)} %subtract_bitcast_fusion, f32[1,2,8,96,1536]{4,3,2,1,0:T(8,128)} %bitcast.92, f32[1,2,8,96,1536]{4,3,2,1,0:T(8,128)} %bitcast.93, f32[2,2,8,32,1536]{4,3,2,1,0:T(8,128)} %fusion.28, ...), kind=kOutput, calls=%fused_computation.12 | convolution fusion | flops 87015555072 | bytes 66063744 | tf_op jit(solution)/shard_map/fpkqy,yj->fpkqj/dot_general | solution.py:139
  1431.2 99.0 %fusion.19 = f32[2,2,8,96,1536]{4,3,2,1,0:T(8,128)} fusion(f32[2,2,8,96,1536]{4,3,2,1,0:T(8,128)} %fusion.9, f32[1536,1536]{1,0:T(8,128)} %param.15, f32[8,96,1536]{2,1,0:T(8,128)} %broadcast_add_fusion), kind=kOutput, calls=%fused_computation.22 | convolution fusion | flops 86977806336 | bytes 51904512 | tf_op jit(solution)/shard_map/fpkqj,yj->fpkqy/dot_general | solution.py:143
  1530.2 12.6 slice_bitcast_fusion
  (9 shorter events, 0.0 us)
Async XLA Ops:
  0.6 19.5 %copy-start = (bf16[3,192,24,512]{3,2,1,0:T(8,128)(2,1)S(1)}, bf16[3,192,24,512]{3,2,1,0:T(8,128)(2,1)}, u32[]{:S(2)}) copy-start(bf16[3,192,24,512]{3,2,1,0:T(8,128)(2,1)} %param.9) | copy-start | bytes 42467332
  156.3 316.8 %all-to-all-start = ((f32[4,3,192,24,128]{4,3,2,1,0:T(8,128)}), f32[4,3,192,24,128]{4,3,2,1,0:T(8,128)}, u32[]{:S(2)}, u32[]{:S(2)}) async-start(f32[4,3,192,24,128]{4,3,2,1,0:T(8,128)} %pad_maximum_fusion), calls=%async_computation | async-start | bytes 56623104 | tf_op jit(solution)/shard_map/all_to_all | solution.py:106
  642.6 6.6 copy-start.3
  642.6 6.7 copy-start.1
  642.6 7.0 copy-start.2
  642.6 550.0 %all-to-all-start.1 = ((f32[3,2,64,64,192]{4,3,1,0,2:T(8,128)}), f32[3,2,64,64,192]{4,3,1,0,2:T(8,128)}, u32[]{:S(2)}, u32[]{:S(2)}) async-start(f32[3,2,64,64,192]{4,3,1,0,2:T(8,128)} %copy.22), calls=%async_computation.1 | async-start | bytes 50331648 | tf_op jit(solution)/shard_map/all_to_all | solution.py:124
